TPU v7x, 32 devices: a whole 2x2x4 slice. The times are simulated.
32 devices in a mesh: groups: 2 (over x), ctx: 8 (over z, y), exp: 2 (over core).
Axes of the slice: x: 2, y: 2, z: 4, core: 2. Of those that a mesh axis runs over, the one named last changes fastest.
Arguments:
- query_states: bfloat16 [1024, 3072], P(('groups', 'ctx'), 'exp'), parts along dimension 0, may hold values from -5 to 5
- key_states: bfloat16 [1024, 512], P(('groups', 'ctx'), 'exp'), parts along dimension 0, may hold values from -5 to 5
- value_states: bfloat16 [1024, 512], P(('groups', 'ctx'), 'exp'), parts along dimension 0, may hold values from -6 to 6
- residual: bfloat16 [1024, 3072], P(('groups', 'ctx'), 'exp'), parts along dimension 0, may hold values from -2 to 2
- norm_gain: float32 [3072], replicated, may hold values from 0.1 to 1.9
- expert_ids: int32 [1024, 2], P(('groups', 'ctx')), parts along dimension 0, may hold values from 0 to 7, all different within a row; in each aligned block of 32 rows (0 to 31, 32 to 63, ...) at most 12 rows name the same one
- route_weights: float32 [1024, 2], P(('groups', 'ctx')), parts along dimension 0, may hold values from 0.1 to 1
- w_gate: bfloat16 [3072, 16384], P(None, ('ctx', 'exp')), may hold values from -0.109375 to 0.109375
- w_down: bfloat16 [16384, 3072], P(('ctx', 'exp')), may hold values from -0.125 to 0.125
Outputs:
- mixed: bfloat16 [1024, 3072], P(('groups', 'ctx'), 'exp'), parts along dimension 0
There are 2 independent parts, one for each index of `groups`. A program takes and returns all parts, laid end to end along the dimension named above; an argument that names none is the same for every part. Nothing has to cross between parts.
Inputs may be any that keep to these rules, and one draw needn't show every extreme that they name: `expert_ids`: each token names 2 different experts. In each aligned block of 32 tokens, at most 12 tokens name the same expert.
All inputs are finite; a program needn't handle non-finite values.
Results may differ from a plain program's by a relative error of at most 0.012.
Values may be sent and summed in bfloat16 or wider, within the bound.
A program may use at most 64 MiB of HBM per device.

v0:
```python
import jax
import jax.numpy as jnp
from jax import lax
from jax.sharding import PartitionSpec as P

D = 3072
HEAD_DIM = 128
EXPERTS = 8
HALF_CAP = 12


def body(
    query_states,
    key_states,
    value_states,
    residual,
    norm_gain,
    expert_ids,
    route_weights,
    w_gate,
    w_down,
):
    n_ctx = lax.axis_size("ctx")
    ctx_rank = lax.axis_index("ctx")
    tok_count = query_states.shape[0]
    kv_local = key_states.shape[1] // HEAD_DIM
    q_local = query_states.shape[1] // HEAD_DIM
    per_group = q_local // kv_local
    query_heads = query_states.reshape(tok_count, kv_local, per_group, HEAD_DIM)
    query_pos = ctx_rank * tok_count + jnp.arange(tok_count, dtype=jnp.int32)
    scaling = HEAD_DIM ** (-0.5)
    row_max = jnp.full((tok_count, kv_local, per_group), -1e30, jnp.float32)
    key_block = lax.all_gather(key_states, "ctx", axis=0, tiled=True)
    value_block = lax.all_gather(value_states, "ctx", axis=0, tiled=True)
    block_rows = key_block.shape[0]
    key_heads = key_block.reshape(block_rows, kv_local, HEAD_DIM)
    value_heads = value_block.reshape(block_rows, kv_local, HEAD_DIM)
    scores = (
        jnp.einsum("qgjd,kgd->qgjk", query_heads, key_heads, preferred_element_type=jnp.float32)
        * scaling
    )
    key_pos = jnp.arange(block_rows, dtype=jnp.int32)
    allowed = (key_pos[None, :] <= query_pos[:, None])[:, None, None, :]
    block_max = jnp.max(jnp.where(allowed, scores, -jnp.inf), axis=-1)
    new_max = jnp.maximum(row_max, block_max)
    expo_terms = jnp.where(allowed, jnp.exp(scores - new_max[..., None]), 0.0)
    new_sum = jnp.sum(expo_terms, axis=-1)
    weighted = jnp.einsum(
        "qgjk,kgd->qgjd",
        expo_terms.astype(jnp.bfloat16),
        value_heads,
        preferred_element_type=jnp.float32,
    )
    attended = (weighted / new_sum[..., None]).reshape(tok_count, q_local * HEAD_DIM)
    hidden_half = (residual.astype(jnp.float32) + attended).astype(jnp.bfloat16)
    feat_half = hidden_half.shape[1]
    choices_per = expert_ids.shape[1]
    capacity = 2 * HALF_CAP
    slot_count = EXPERTS * capacity
    spread = n_ctx // EXPERTS
    hit_table = (
        expert_ids[:, :, None] == jnp.arange(EXPERTS, dtype=jnp.int32)[None, None, :]
    ).astype(jnp.int32)
    blocks = hit_table.reshape(2, tok_count // 2 * choices_per, EXPERTS)
    earlier = jnp.cumsum(blocks, axis=1) - blocks
    slot_table = (
        jnp.arange(EXPERTS, dtype=jnp.int32)[None, None, :] * capacity
        + jnp.arange(2, dtype=jnp.int32)[:, None, None] * HALF_CAP
        + earlier
    )
    slot_of = jnp.sum(blocks * slot_table, axis=2).reshape(tok_count, choices_per)
    slot_marks = slot_of[:, :, None] == jnp.arange(slot_count, dtype=jnp.int32)[None, None, :]
    placing = jnp.any(slot_marks, axis=1).astype(jnp.bfloat16)
    combine = jnp.sum(jnp.where(slot_marks, route_weights[:, :, None], 0.0), axis=1)
    half_float = hidden_half.astype(jnp.float32)
    squares = lax.psum(jnp.sum(jnp.square(half_float), axis=1), "exp")
    inv_rms = lax.rsqrt(squares / D + 1e-05)
    gain_half = lax.dynamic_slice_in_dim(norm_gain, lax.axis_index("exp") * feat_half, feat_half)
    normed_half = (half_float * inv_rms[:, None] * gain_half[None, :]).astype(jnp.bfloat16)
    sent_rows = jnp.einsum(
        "ts,td->sd", placing, normed_half, preferred_element_type=jnp.float32
    ).astype(jnp.bfloat16)
    whole_rows = lax.all_gather(
        lax.all_to_all(
            jnp.repeat(sent_rows.reshape(EXPERTS, capacity, normed_half.shape[1]), spread, axis=0),
            "ctx",
            split_axis=0,
            concat_axis=0,
            tiled=True,
        ),
        "exp",
        axis=2,
        tiled=True,
    )
    flat_rows = whole_rows.reshape(whole_rows.shape[0] * whole_rows.shape[1], whole_rows.shape[2])
    gate_act = jax.nn.silu(jnp.dot(flat_rows, w_gate, preferred_element_type=jnp.float32)).astype(
        jnp.bfloat16
    )
    partial_value = jnp.dot(gate_act, w_down, preferred_element_type=jnp.float32)
    computed = lax.psum_scatter(
        partial_value.reshape(
            whole_rows.shape[0], whole_rows.shape[1], partial_value.shape[1]
        ).astype(jnp.bfloat16),
        "exp",
        scatter_dimension=2,
        tiled=True,
    ).astype(jnp.float32)
    returned = lax.all_to_all(
        computed.astype(jnp.bfloat16), "ctx", split_axis=0, concat_axis=0, tiled=True
    ).astype(computed.dtype)
    summed = jnp.sum(returned.reshape(EXPERTS, spread, capacity, returned.shape[2]), axis=1)
    summed = summed.reshape(slot_count, returned.shape[2])
    branch = jnp.dot(
        combine, summed, precision=lax.Precision.HIGHEST, preferred_element_type=jnp.float32
    )
    return (hidden_half.astype(jnp.float32) + branch).astype(jnp.bfloat16)


def solution(mesh):
    in_specs = (
        P(("groups", "ctx"), "exp"),
        P(("groups", "ctx"), "exp"),
        P(("groups", "ctx"), "exp"),
        P(("groups", "ctx"), "exp"),
        P(),
        P(("groups", "ctx"), None),
        P(("groups", "ctx"), None),
        P(None, ("ctx", "exp")),
        P(("ctx", "exp"), None),
    )
    out_specs = P(("groups", "ctx"), "exp")
    return jax.shard_map(body, mesh=mesh, in_specs=in_specs, out_specs=out_specs, check_vma=False)
```

profile of v0, /device:TPU:0, one launch (start us, length us, event | category | flops | bytes accessed | tf_op | source)
XLA Modules:
  0.0 156.8 jit_solution(8592086809740125504)
XLA Ops:
  6.5 0.0 all-gather.2.cloned.1.call-start
  6.5 0.1 iota_compare_fusion.1
  6.6 32.8 %all_gather.9 = bf16[512,256]{1,0:T(8,128)(2,1)S(1)} all-gather(bf16[64,256]{1,0:T(8,128)(2,1)} %param.10), channel_id=1, replica_groups=mesh['groups'=2,'ctx'=8,'exp'=2] {'ctx'}, dimensions={0}, use_global_device_ids=true | all-gather | bytes 294912 | tf_op jit(solution)/shard_map/all_gather | solution.py:33
  39.4 0.0 copy-start.1
  39.4 0.1 copy.29
  39.6 1.2 reshape.98
  40.7 0.4 fusion.1
  41.2 0.0 copy-done.1
  41.2 30.7 %all_gather.10 = bf16[512,256]{1,0:T(8,128)(2,1)S(1)} all-gather(bf16[64,256]{1,0:T(8,128)(2,1)S(1)} %copy-done.1), channel_id=1, replica_groups=mesh['groups'=2,'ctx'=8,'exp'=2] {'ctx'}, dimensions={0}, use_global_device_ids=true | all-gather | bytes 294912 | tf_op jit(solution)/shard_map/all_gather | solution.py:34
  71.9 0.1 copy.32
  72.1 0.5 fusion.4
  72.6 0.5 fusion.6
  73.1 0.0 copy-start
  73.1 0.0 copy-start.4
  73.1 0.0 copy-start.2
  73.1 0.2 copy.34
  73.4 0.1 reshape.100
  73.5 0.5 copy-done
  74.0 0.2 fusion.11
  74.2 2.5 %psum.7 = f32[64]{0:T(128)S(1)} all-reduce(f32[64]{0:T(128)S(1)} %get-tuple-element.5), channel_id=1, replica_groups=mesh['groups'=2,'ctx'=8,'exp'=2] {'exp'}, use_global_device_ids=true, to_apply=%region_7.8 | all-reduce | flops 64 | bytes 512 | tf_op jit(solution)/shard_map/psum | solution.py:76
  76.6 0.0 copy-done.4
  76.6 0.1 copy.35
  76.7 0.1 eq.31
  76.9 0.1 fusion.20
  77.0 0.1 reduce_window_sum.11
  77.1 0.1 broadcast_add_fusion
  77.1 0.2 select_reduce_fusion.1
  77.3 0.1 eq.35
  77.4 0.1 copy.36
  77.5 0.1 fusion.19
  77.6 0.0 copy-done.2
  77.6 0.1 dynamic_slice.3
  77.7 0.4 convolution_convert_fusion.1
  78.1 22.4 %all_to_all.10 = bf16[8,24,1536]{2,1,0:T(8,128)(2,1)} all-to-all(bf16[8,24,1536]{2,1,0:T(8,128)(2,1)S(1)} %bitcast.41), channel_id=1, replica_groups=mesh['groups'=2,'ctx'=8,'exp'=2] {'ctx'}, dimensions={0} | all-to-all | bytes 1179648 | tf_op jit(solution)/shard_map/all_to_all | solution.py:84
  100.4 0.0 all-gather.2.cloned.1.call-update
  100.5 0.0 reduce-scatter.2.cloned.1.call-start
  100.5 7.7 %all-gather.2.cloned.1.call-done = bf16[8,24,3072]{2,1,0:T(8,128)(2,1)} async-done(((bf16[8,24,1536]{2,1,0:T(8,128)(2,1)}), bf16[8,24,3072]{2,1,0:T(8,128)(2,1)}) %all-gather.2.cloned.1.call-update) | async-done | bytes 1179664 | tf_op jit(solution)/shard_map/all_gather | solution.py:83
  108.3 8.7 %convolution_convert_fusion = bf16[192,3072]{1,0:T(8,128)(2,1)} fusion(bf16[1024,3072]{1,0:T(8,128)(2,1)} %param.17, bf16[192,3072]{1,0:T(8,128)(2,1)} %bitcast.45, bf16[3072,1024]{1,0:T(8,128)(2,1)} %param.16), kind=kOutput, calls=%fused_computation | convolution fusion | flops 2417491968 | bytes 14942208 | tf_op jit(solution)/shard_map/dot_general | solution.py:99
  116.9 0.0 copy-start.3
  116.9 0.0 reduce-scatter.2.cloned.1.call-update
  116.9 9.8 %reduce-scatter.2.cloned.1.call-done = bf16[8,24,1536]{2,1,0:T(8,128)(2,1)} async-done(((bf16[8,24,3072]{2,1,0:T(8,128)(2,1)}), bf16[8,24,1536]{2,1,0:T(8,128)(2,1)}) %reduce-scatter.2.cloned.1.call-update) | async-done | bytes 589840 | tf_op jit(solution)/shard_map/reduce_scatter | solution.py:100
  126.7 5.9 %all-to-all-start.1 = ((bf16[8,24,1536]{2,1,0:T(8,128)(2,1)}), bf16[8,24,1536]{2,1,0:T(8,128)(2,1)S(1)}, u32[]{:S(2)}, u32[]{:S(2)}) async-start(bf16[8,24,1536]{2,1,0:T(8,128)(2,1)} %reduce-scatter.2.cloned.1.call-done), calls=%async_computation.2 | async-start | bytes 1179648 | tf_op jit(solution)/shard_map/all_to_all | solution.py:108
  132.6 0.0 copy-done.3
  132.6 0.1 select_reduce_fusion
  132.7 16.2 %all-to-all-done.1 = bf16[8,24,1536]{2,1,0:T(8,128)(2,1)S(1)} async-done(((bf16[8,24,1536]{2,1,0:T(8,128)(2,1)}), bf16[8,24,1536]{2,1,0:T(8,128)(2,1)S(1)}, u32[]{:S(2)}, u32[]{:S(2)}) %all-to-all-start.1) | async-done | bytes 589856 | tf_op jit(solution)/shard_map/all_to_all | solution.py:108
  148.9 1.1 fusion
  (5 shorter events, 0.0 us)
Async XLA Ops:
  6.5 101.7 %all-gather.2.cloned.1.call-start = ((), (), s32[]{:S(2)}) async-start(), calls=%async_computation.3 | async-start | bytes 1769472 | tf_op jit(solution)/shard_map/all_gather | solution.py:83
  39.4 1.8 %copy-start.1 = (bf16[64,256]{1,0:T(8,128)(2,1)S(1)}, bf16[64,256]{1,0:T(8,128)(2,1)}, u32[]{:S(2)}) copy-start(bf16[64,256]{1,0:T(8,128)(2,1)} %param.11) | copy-start | bytes 98308
  73.1 0.9 copy-start
  73.1 3.6 %copy-start.4 = (s32[64,2]{0,1:T(2,128)S(1)}, s32[64,2]{0,1:T(2,128)}, u32[]{:S(2)}) copy-start(s32[64,2]{0,1:T(2,128)} %param.14) | copy-start | bytes 1540
  73.1 4.5 %copy-start.2 = (f32[3072]{0:T(1024)S(1)}, f32[3072]{0:T(1024)}, u32[]{:S(2)}) copy-start(f32[3072]{0:T(1024)} %param.13) | copy-start | bytes 36868
  100.5 26.3 %reduce-scatter.2.cloned.1.call-start = ((), (), s32[]{:S(2)}) async-start(), calls=%async_computation.4 | async-start | bytes 1769472 | tf_op jit(solution)/shard_map/reduce_scatter | solution.py:100
  116.9 15.7 %copy-start.3 = (f32[64,2]{0,1:T(2,128)S(1)}, f32[64,2]{0,1:T(2,128)}, u32[]{:S(2)}) copy-start(f32[64,2]{0,1:T(2,128)} %param.15) | copy-start | bytes 1540
  126.7 22.2 %all-to-all-start.1 = ((bf16[8,24,1536]{2,1,0:T(8,128)(2,1)}), bf16[8,24,1536]{2,1,0:T(8,128)(2,1)S(1)}, u32[]{:S(2)}, u32[]{:S(2)}) async-start(bf16[8,24,1536]{2,1,0:T(8,128)(2,1)} %reduce-scatter.2.cloned.1.call-done), calls=%async_computation.2 | async-start | bytes 1179648 | tf_op jit(solution)/shard_map/all_to_all | solution.py:108
Sparse Core Ops, SparseCore 0:
  100.6 7.6 all-gather.1
  117.0 9.6 reduce-scatter.1
where the time goes:
time: 157 us
  blocking collectives  88.3 us (56%)
  waiting for transfers between devices  33.8 us (22%)
  between operations  13.5 us (9%)
  matrix products  11.1 us (7%)
  starting transfers between devices  5.91 us (4%)
  local copies, waits for them, and re-layouts  2.82 us (2%)
    all_gather x1, blocking collectives, body(): key_block = lax.all_gather(key_states, 'ctx', axis=0, tiled=True)  32.8 us
    all_gather x1, blocking collectives, body(): value_block = lax.all_gather(value_states, 'ctx', axis=0, tiled=True)  30.7 us
    all_to_all x1, blocking collectives, body(): lax.all_to_all(jnp.repeat(sent_rows.reshape(EXPERTS, capacity, normed_hal...  22.4 us
    all_to_all x1, waiting for transfers between devices, body(): lax.all_to_all(computed.astype(jnp.bfloat16), 'ctx', split_axis=0, concat...  16.2 us
    reduce_scatter x1, waiting for transfers between devices, body(): lax.psum_scatter(partial_value.reshape(whole_rows.shape[0], whole_rows.sh...  9.82 us
    dot_general x1, matrix products, body(): jnp.dot(gate_act, w_down, preferred_element_type=jnp.float32)  8.65 us
    all_gather x1, waiting for transfers between devices, body(): lax.all_gather(lax.all_to_all(jnp.repeat(sent_rows.reshape(EXPERTS, capac...  7.74 us
    all_to_all x1, starting transfers between devices, body(): lax.all_to_all(computed.astype(jnp.bfloat16), 'ctx', split_axis=0, concat...  5.87 us
  transfers between devices with their start and end apart: 3, of which 3 were waited for; matrix products, arithmetic and copies ran while one was open for 0% of the time, Pallas kernels for 0%

commit v1 on v0

v1 whole, which is shorter than its diff:
```python
import functools

import jax
import jax.numpy as jnp
from jax import lax
from jax.experimental import pallas as pl
from jax.experimental.pallas import tpu as pltpu
from jax.sharding import PartitionSpec as P

HEAD_DIM = 128
EXPERTS = 8
HALF_CAP = 12
CAP = 2 * HALF_CAP
CHUNK = 512
MESH = pl.DeviceIdType.MESH
F32 = jnp.float32
BF16 = jnp.bfloat16


def kernel(
    n,
    q_ref, k_ref, v_ref, res_ref, gain_ref, ids_ref, rw_ref, wg_hbm, wd_hbm,
    out_ref,
    kbuf, vbuf, wg, wd, hid, place, comb, sq_send, sq_recv,
    send_buf, recv_own, recv_sib, lhs_own, lhs_sib, acc, act,
    psend, precv, rsend, rrecv,
    w_sem, kv_send, kv_recv, sq_sem, disp_send, disp_recv, sib_send, sib_recv,
    p_send, p_recv, r_send, r_recv,
):
    me = lax.axis_index("ctx")
    x = lax.axis_index("exp")
    sib = 1 - x
    toks = q_ref.shape[0]
    half_feat = q_ref.shape[1]
    kv_local = k_ref.shape[1] // HEAD_DIM
    per_group = half_feat // HEAD_DIM // kv_local
    spread = n // EXPERTS
    slots = EXPERTS * CAP
    chunks = half_feat // CHUNK
    nz = n // 2
    rows = n * CAP
    ff = wg.shape[1]

    wg_copy = pltpu.make_async_copy(wg_hbm, wg, w_sem.at[0])
    wd_copy = pltpu.make_async_copy(wd_hbm, wd, w_sem.at[1])
    wg_copy.start()
    wd_copy.start()

    barrier = pltpu.get_barrier_semaphore()
    for d in range(1, n):
        pl.semaphore_signal(
            barrier, inc=1, device_id={"ctx": lax.rem(me + d, n)}, device_id_type=MESH
        )
    pl.semaphore_signal(barrier, inc=1, device_id={"exp": sib}, device_id_type=MESH)
    pl.semaphore_wait(barrier, n)

    parity = lax.rem(me, 2)
    level = lax.div(me, 2)
    partner = me + 1 - 2 * parity
    bufs = (kbuf, vbuf)

    def kv_copy(i, src, block, dst, slot):
        return pltpu.make_async_remote_copy(
            src_ref=src,
            dst_ref=bufs[i].at[block],
            send_sem=kv_send.at[i, slot],
            recv_sem=kv_recv.at[i, block],
            device_id={"ctx": dst},
            device_id_type=MESH,
        )

    def own_copies(dst, slot):
        return [kv_copy(i, (k_ref, v_ref)[i], me, dst, slot) for i in range(2)]

    def relay_copies(block, slot):
        return [kv_copy(i, bufs[i].at[block], block, partner, slot) for i in range(2)]

    @pl.when(parity == 0)
    def _():
        for c in own_copies(partner, 0):
            c.start()

    for dz in range(1, nz):
        @pl.when(level + dz < nz)
        def _():
            for c in own_copies(me + 2 * dz, dz):
                c.start()

    kbuf[me] = k_ref[...]
    vbuf[me] = v_ref[...]
    for b in range(n):
        @pl.when(b > me)
        def _():
            kbuf[b] = jnp.zeros(k_ref.shape, BF16)
            vbuf[b] = jnp.zeros(v_ref.shape, BF16)

    slot = lax.broadcasted_iota(jnp.int32, (toks, slots), 1)
    expert = jnp.zeros((toks, slots), jnp.int32)
    for e in range(1, EXPERTS):
        expert = expert + (slot >= e * CAP).astype(jnp.int32)
    pos = slot - expert * CAP
    token = lax.broadcasted_iota(jnp.int32, (toks, slots), 0)
    block_len = toks // 2
    in_second = (token >= block_len).astype(jnp.int32)
    ids = ids_ref[...]
    rw = rw_ref[...]
    first = jnp.where(ids[:, 0:1] == expert, 1.0, 0.0)
    second = jnp.where(ids[:, 1:2] == expert, 1.0, 0.0)
    chosen = first + second
    t_row = lax.broadcasted_iota(jnp.int32, (toks, toks), 0)
    t_col = lax.broadcasted_iota(jnp.int32, (toks, toks), 1)
    same = (t_row >= block_len) == (t_col >= block_len)
    lower = jnp.where(same & (t_col < t_row), 1.0, 0.0).astype(BF16)
    rank = jnp.dot(lower, chosen.astype(BF16), preferred_element_type=F32)
    wanted = (pos - in_second * HALF_CAP).astype(F32)
    placing = jnp.where(rank == wanted, chosen, 0.0)
    place[...] = placing
    weight = placing * (first * rw[:, 0:1] + second * rw[:, 1:2])
    high = weight.astype(BF16)
    comb[0:toks, :] = high
    comb[toks:, :] = (weight - high.astype(F32)).astype(BF16)

    for dz in range(1, nz):
        @pl.when(level - dz >= 0)
        def _():
            block = me - 2 * dz
            for c in relay_copies(block, nz + dz - 1):
                c.wait_recv()
                c.start()
    for j in range(nz):
        block = 2 * j + 1 - parity

        @pl.when(block < me)
        def _():
            for c in relay_copies(block, 0):
                c.wait_recv()

    keys = n * toks
    q_pos = me * toks + lax.broadcasted_iota(jnp.int32, (toks, keys), 0)
    k_pos = lax.broadcasted_iota(jnp.int32, (toks, keys), 1)
    bias = jnp.where(k_pos <= q_pos, 0.0, -1e30)
    bias = jnp.concatenate([bias] * per_group, axis=0)
    scaling = HEAD_DIM ** (-0.5)
    squares = jnp.zeros((toks, 1), F32)
    for g in range(kv_local):
        head = slice(g * HEAD_DIM, (g + 1) * HEAD_DIM)
        base = g * per_group * HEAD_DIM
        qs = jnp.concatenate(
            [
                q_ref[:, base + j * HEAD_DIM : base + (j + 1) * HEAD_DIM]
                for j in range(per_group)
            ],
            axis=0,
        )
        ks = kbuf[:, :, head].reshape(keys, HEAD_DIM)
        vs = vbuf[:, :, head].reshape(keys, HEAD_DIM)
        s = lax.dot_general(qs, ks, (((1,), (1,)), ((), ())), preferred_element_type=F32)
        s = s * scaling + bias
        m = jnp.max(s, axis=1, keepdims=True)
        p = jnp.exp(s - m)
        total = jnp.sum(p, axis=1, keepdims=True)
        att = jnp.dot(p.astype(BF16), vs, preferred_element_type=F32) / total
        for j in range(per_group):
            cols = slice(base + j * HEAD_DIM, base + (j + 1) * HEAD_DIM)
            h = (res_ref[:, cols].astype(F32) + att[j * toks : (j + 1) * toks]).astype(BF16)
            hid[:, cols] = h
            squares = squares + jnp.sum(jnp.square(h.astype(F32)), axis=1, keepdims=True)

    sq_send[...] = jnp.broadcast_to(squares, sq_send.shape)
    sq_copy = pltpu.make_async_remote_copy(
        src_ref=sq_send, dst_ref=sq_recv, send_sem=sq_sem.at[0], recv_sem=sq_sem.at[1],
        device_id={"exp": sib}, device_id_type=MESH,
    )
    sq_copy.start()
    my_feat = pl.multiple_of(x * half_feat, half_feat)
    sib_feat = pl.multiple_of(sib * half_feat, half_feat)
    gain = gain_ref[:, pl.ds(my_feat, half_feat)]
    scaled = hid[...].astype(F32)
    sq_copy.wait()
    inv = lax.rsqrt((squares + sq_recv[:, 0:1]) / (2 * half_feat) + 1e-05)
    normed = (scaled * inv * gain).astype(BF16)

    sent = lax.dot_general(
        place[...].astype(BF16), normed, (((0,), (0,)), ((), ())), preferred_element_type=F32
    )
    send_buf[...] = sent.reshape(EXPERTS, CAP, half_feat).astype(BF16)
    my_expert = lax.div(me, spread)

    def disp_copy(dst, block, src_expert, slot):
        return pltpu.make_async_remote_copy(
            src_ref=send_buf.at[src_expert], dst_ref=recv_own.at[block],
            send_sem=disp_send.at[slot], recv_sem=disp_recv.at[block],
            device_id={"ctx": dst}, device_id_type=MESH,
        )

    def sib_copy(src, block):
        return pltpu.make_async_remote_copy(
            src_ref=src, dst_ref=recv_sib.at[block],
            send_sem=sib_send.at[block], recv_sem=sib_recv.at[block],
            device_id={"exp": sib}, device_id_type=MESH,
        )

    for d in range(1, n):
        dst = lax.rem(me + d, n)
        disp_copy(dst, me, lax.div(dst, spread), d).start()
    sib_copy(send_buf.at[my_expert], me).start()
    recv_own[me] = send_buf[my_expert]
    for d in range(1, n):
        src = lax.rem(me - d + n, n)
        disp_copy(src, src, my_expert, d).wait_recv()
        sib_copy(recv_own.at[src], src).start()

    lhs_own[...] = recv_own[...].astype(F32).reshape(rows, half_feat).astype(BF16)
    wg_copy.wait()
    for c in range(ff // 256):
        cols = slice(c * 256, (c + 1) * 256)
        acc[:, cols] = jnp.dot(
            lhs_own[...], wg[pl.ds(my_feat, half_feat), cols], preferred_element_type=F32
        )
    for d in range(n):
        sib_copy(send_buf.at[0], lax.rem(me - d + n, n)).wait_recv()
    lhs_sib[...] = recv_sib[...].astype(F32).reshape(rows, half_feat).astype(BF16)
    for c in range(ff // 256):
        cols = slice(c * 256, (c + 1) * 256)
        v = acc[:, cols] + jnp.dot(
            lhs_sib[...], wg[pl.ds(sib_feat, half_feat), cols], preferred_element_type=F32
        )
        act[:, cols] = (v / (1.0 + jnp.exp(-v))).astype(BF16)

    def p_copy(j):
        return pltpu.make_async_remote_copy(
            src_ref=psend.at[j], dst_ref=precv.at[j],
            send_sem=p_send.at[j], recv_sem=p_recv.at[j],
            device_id={"exp": sib}, device_id_type=MESH,
        )

    def r_copy(j, dst, block, slot):
        return pltpu.make_async_remote_copy(
            src_ref=rsend.at[j, dst], dst_ref=rrecv.at[j, block],
            send_sem=r_send.at[j, slot], recv_sem=r_recv.at[j, block],
            device_id={"ctx": dst}, device_id_type=MESH,
        )

    wd_copy.wait()
    for j in range(chunks):
        cols = pl.ds(pl.multiple_of(sib_feat + j * CHUNK, CHUNK), CHUNK)
        y = jnp.dot(act[...], wd[:, cols], preferred_element_type=F32)
        psend[j] = y.reshape(n, CAP, CHUNK).astype(BF16)
        p_copy(j).start()
    for j in range(chunks):
        cols = pl.ds(pl.multiple_of(my_feat + j * CHUNK, CHUNK), CHUNK)
        y = jnp.dot(act[...], wd[:, cols], preferred_element_type=F32)
        p_copy(j).wait_recv()
        rsend[j] = (y.reshape(n, CAP, CHUNK) + precv[j].astype(F32)).astype(BF16)
        for d in range(1, n):
            r_copy(j, lax.rem(me + d, n), me, d).start()
        rrecv[j, me] = rsend[j, me]

    for j in range(chunks):
        for d in range(1, n):
            src = lax.rem(me - d + n, n)
            r_copy(j, src, src, d).wait_recv()
        back = rrecv[j].astype(F32).reshape(EXPERTS, spread, CAP, CHUNK)
        if spread == 1:
            back = back.reshape(slots, CHUNK).astype(BF16)
            both = jnp.dot(comb[...], back, preferred_element_type=F32)
        else:
            back = jnp.sum(back, axis=1).reshape(slots, CHUNK)
            top = back.astype(BF16)
            rest = (back - top.astype(F32)).astype(BF16)
            both = jnp.dot(comb[...], top, preferred_element_type=F32)
            both = both + jnp.dot(comb[...], rest, preferred_element_type=F32)
        cols = slice(j * CHUNK, (j + 1) * CHUNK)
        mixed = hid[:, cols].astype(F32) + both[:toks] + both[toks:]
        out_ref[:, cols] = mixed.astype(BF16)

    @pl.when(parity == 0)
    def _():
        for c in own_copies(partner, 0):
            c.wait_send()

    for dz in range(1, nz):
        @pl.when(level + dz < nz)
        def _():
            for c in own_copies(me + 2 * dz, dz):
                c.wait_send()

        @pl.when(level - dz >= 0)
        def _():
            for c in relay_copies(me - 2 * dz, nz + dz - 1):
                c.wait_send()

    for d in range(1, n):
        dst = lax.rem(me + d, n)
        disp_copy(dst, me, lax.div(dst, spread), d).wait_send()
    for d in range(n):
        sib_copy(send_buf.at[0], lax.rem(me - d + n, n)).wait_send()
    for j in range(chunks):
        p_copy(j).wait_send()
        for d in range(1, n):
            r_copy(j, lax.rem(me + d, n), me, d).wait_send()


def solution(mesh):
    n = mesh.shape["ctx"]

    def body(q, k, v, res, gain, ids, rw, w_gate, w_down):
        toks, half_feat = q.shape
        ff = w_gate.shape[1]
        rows = n * CAP
        slots = EXPERTS * CAP
        chunks = half_feat // CHUNK
        dma = pltpu.SemaphoreType.DMA
        vmem = pl.BlockSpec(memory_space=pltpu.VMEM)
        anyspace = pl.BlockSpec(memory_space=pl.ANY)
        return pl.pallas_call(
            functools.partial(kernel, n),
            out_shape=jax.ShapeDtypeStruct((toks, half_feat), BF16),
            in_specs=[vmem] * 7 + [anyspace] * 2,
            out_specs=vmem,
            scratch_shapes=[
                pltpu.VMEM((n, toks, k.shape[1]), BF16),
                pltpu.VMEM((n, toks, k.shape[1]), BF16),
                pltpu.VMEM(w_gate.shape, BF16),
                pltpu.VMEM(w_down.shape, BF16),
                pltpu.VMEM((toks, half_feat), BF16),
                pltpu.VMEM((toks, slots), F32),
                pltpu.VMEM((2 * toks, slots), BF16),
                pltpu.VMEM((toks, 128), F32),
                pltpu.VMEM((toks, 128), F32),
                pltpu.VMEM((EXPERTS, CAP, half_feat), BF16),
                pltpu.VMEM((n, CAP, half_feat), BF16),
                pltpu.VMEM((n, CAP, half_feat), BF16),
                pltpu.VMEM((rows, half_feat), BF16),
                pltpu.VMEM((rows, half_feat), BF16),
                pltpu.VMEM((rows, ff), F32),
                pltpu.VMEM((rows, ff), BF16),
                pltpu.VMEM((chunks, n, CAP, CHUNK), BF16),
                pltpu.VMEM((chunks, n, CAP, CHUNK), BF16),
                pltpu.VMEM((chunks, n, CAP, CHUNK), BF16),
                pltpu.VMEM((chunks, n, CAP, CHUNK), BF16),
                dma((2,)),
                dma((2, n)),
                dma((2, n)),
                dma((2,)),
                dma((n,)),
                dma((n,)),
                dma((n,)),
                dma((n,)),
                dma((chunks,)),
                dma((chunks,)),
                dma((chunks, n)),
                dma((chunks, n)),
            ],
            compiler_params=pltpu.CompilerParams(
                collective_id=0, has_side_effects=True, vmem_limit_bytes=60 * 1024 * 1024
            ),
        )(q, k, v, res, gain.reshape(1, -1), ids, rw, w_gate, w_down)

    rows_spec = P(("groups", "ctx"), "exp")
    in_specs = (
        rows_spec, rows_spec, rows_spec, rows_spec, P(),
        P(("groups", "ctx"), None), P(("groups", "ctx"), None),
        P(None, ("ctx", "exp")), P(("ctx", "exp"), None),
    )
    return jax.shard_map(
        body, mesh=mesh, in_specs=in_specs, out_specs=rows_spec, check_vma=False
    )
```

time: 157 us -> 56.3 us (0.36)
  blocking collectives: 88.3 us -> 0 us
  Pallas kernels: 0 us -> 51.7 us
  waiting for transfers between devices: 33.8 us -> 0 us
  between operations: 13.5 us -> 0.01 us
  matrix products: 11.1 us -> 0 us
  starting transfers between devices: 5.91 us -> 0 us
    all_gather x2 -> x0, blocking collectives: 63.5 us -> none  [the longest x1 32.8 us: body(): key_block = lax.all_gather(key_states, 'ctx', axis=0, tiled=True)]
    pallas_call x0 -> x1, Pallas kernels: none -> 51.7 us  [body(): pl.pallas_call(functools.partial(kernel, n), out_shape=jax.ShapeDtypeStru...]
    all_to_all x1 -> x0, blocking collectives: 22.4 us -> none  [body(): lax.all_to_all(jnp.repeat(sent_rows.reshape(EXPERTS, capacity, normed_hal...]
    all_to_all x1 -> x0, waiting for transfers between devices: 16.2 us -> none  [body(): lax.all_to_all(computed.astype(jnp.bfloat16), 'ctx', split_axis=0, concat...]
    dot_general x5 -> x0, matrix products: 11.1 us -> none  [the longest x1 8.65 us: body(): jnp.dot(gate_act, w_down, preferred_element_type=jnp.float32)]
    reduce_scatter x1 -> x0, waiting for transfers between devices: 9.82 us -> none  [body(): lax.psum_scatter(partial_value.reshape(whole_rows.shape[0], whole_rows.sh...]
    all_gather x1 -> x0, waiting for transfers between devices: 7.74 us -> none  [body(): lax.all_gather(lax.all_to_all(jnp.repeat(sent_rows.reshape(EXPERTS, capac...]
    all_to_all x1 -> x0, starting transfers between devices: 5.87 us -> none  [body(): lax.all_to_all(computed.astype(jnp.bfloat16), 'ctx', split_axis=0, concat...]
  transfers between devices with their start and end apart: 3 -> 0, of which waited for: 3 -> 0; matrix products, arithmetic and copies ran while one was open for 0% -> 0% of each run, Pallas kernels for 0% -> 0%
where the time goes in v1:
time: 56.3 us; the launch traced here: 56.1 us
  Pallas kernels  51.7 us (92%)
  local copies, waits for them, and re-layouts  4.36 us (8%)
    pallas_call x1, Pallas kernels, body(): pl.pallas_call(functools.partial(kernel, n), out_shape=jax.ShapeDtypeStru...  51.7 us
    unnamed x3, local copies, waits for them, and re-layouts  4.36 us

profile of v1, /device:TPU:0, one launch (start us, length us, event | category | flops | bytes accessed | tf_op | source)
XLA Modules:
  0.0 56.1 jit_solution(12989605616411615629)
XLA Ops:
  0.0 1.4 %copy.10.ids_ref = s32[64,2]{1,0:T(8,128)} copy(s32[64,2]{0,1:T(2,128)} %param.14) | data formatting | bytes 1024 | tf_op args[5]
  1.4 1.4 %copy.11.rw_ref = f32[64,2]{1,0:T(8,128)} copy(f32[64,2]{0,1:T(2,128)} %param.15) | data formatting | bytes 1024 | tf_op args[6]
  2.7 51.7 %shard_map.91 = bf16[64,1536]{1,0:T(8,128)(2,1)} custom-call(bf16[64,1536]{1,0:T(8,128)(2,1)} %q_ref.1, bf16[64,256]{1,0:T(8,128)(2,1)} %k_ref.1, bf16[64,256]{1,0:T(8,128)(2,1)} %v_ref.1, bf16[64,1536]{1,0:T(8,128)(2,1)} %res_ref.1, f32[1,3072]{1,0:T(1,128)} %bitcast.1, s32[64,2]{1,0:T(8,128)} %copy.10.ids_ref, f32[64,2]{1,0:T(8,128)} %copy.11.rw_ref, ...), custom_call_target="tpu_custom_call" | custom-call | tf_op jit(solution)/shard_map/pallas_call | solution.py:316
  54.5 1.6 %copy.13 = bf16[64,1536]{1,0:T(8,128)(2,1)} copy(bf16[64,1536]{1,0:T(8,128)(2,1)} %shard_map.91) | data formatting | bytes 393216

commit v2 on v1

v2 whole, which is shorter than its diff:
```python
import functools

import jax
import jax.numpy as jnp
from jax import lax
from jax.experimental import pallas as pl
from jax.experimental.pallas import tpu as pltpu
from jax.sharding import PartitionSpec as P

HEAD_DIM = 128
EXPERTS = 8
HALF_CAP = 12
CAP = 2 * HALF_CAP
PARTS = (16, 8)
CHUNK = 768
MESH = pl.DeviceIdType.MESH
F32 = jnp.float32
BF16 = jnp.bfloat16


def kernel(
    n,
    q_ref, k_ref, v_ref, res_ref, gain_ref, ids_ref, rw_ref, wg_hbm, wd_hbm,
    hid, branch,
    kbuf, vbuf, wg, wd, place, comb, sq_send, sq_recv,
    send_a, send_b, own_a, own_b, other_a, other_b, acc, act, flat,
    psend_a, psend_b, precv_a, precv_b, rsend_a, rsend_b, rrecv_a, rrecv_b,
    w_sem, kv_send, kv_recv, sq_sem, disp_send, disp_recv, sib_send, sib_recv,
    p_send, p_recv, r_send, r_recv,
):
    send_buf, recv_own, recv_sib = (send_a, send_b), (own_a, own_b), (other_a, other_b)
    psend, precv = (psend_a, psend_b), (precv_a, precv_b)
    rsend, rrecv = (rsend_a, rsend_b), (rrecv_a, rrecv_b)
    me = lax.axis_index("ctx")
    x = lax.axis_index("exp")
    sib = 1 - x
    toks = q_ref.shape[0]
    half_feat = q_ref.shape[1]
    kv_local = k_ref.shape[1] // HEAD_DIM
    per_group = half_feat // HEAD_DIM // kv_local
    spread = n // EXPERTS
    slots = EXPERTS * CAP
    chunks = half_feat // CHUNK
    nz = n // 2
    ff = wg.shape[1]

    def flip(m):
        other, bit = me, 1
        while bit < n:
            if m & bit:
                other = other + bit * (1 - 2 * lax.rem(lax.div(me, bit), 2))
            bit *= 2
        return other

    order = range(1, n)

    wg_copy = pltpu.make_async_copy(wg_hbm, wg, w_sem.at[0])
    wd_copy = pltpu.make_async_copy(wd_hbm, wd, w_sem.at[1])
    wg_copy.start()
    wd_copy.start()

    barrier = pltpu.get_barrier_semaphore()
    for d in range(1, n):
        pl.semaphore_signal(
            barrier, inc=1, device_id={"ctx": lax.rem(me + d, n)}, device_id_type=MESH
        )
    pl.semaphore_signal(barrier, inc=1, device_id={"exp": sib}, device_id_type=MESH)
    pl.semaphore_wait(barrier, n)

    parity = lax.rem(me, 2)
    level = lax.div(me, 2)
    partner = me + 1 - 2 * parity
    bufs = (kbuf, vbuf)

    def kv_copy(i, src, block, dst, slot):
        return pltpu.make_async_remote_copy(
            src_ref=src,
            dst_ref=bufs[i].at[block],
            send_sem=kv_send.at[i, slot],
            recv_sem=kv_recv.at[i, block],
            device_id={"ctx": dst},
            device_id_type=MESH,
        )

    def own_copies(dst, slot):
        return [kv_copy(i, (k_ref, v_ref)[i], me, dst, slot) for i in range(2)]

    def relay_copies(block, slot):
        return [kv_copy(i, bufs[i].at[block], block, partner, slot) for i in range(2)]

    @pl.when(parity == 0)
    def _():
        for c in own_copies(partner, 0):
            c.start()

    for dz in range(1, nz):
        @pl.when(level + dz < nz)
        def _():
            for c in own_copies(me + 2 * dz, dz):
                c.start()

    kbuf[me] = k_ref[...]
    vbuf[me] = v_ref[...]
    for b in range(n):
        @pl.when(b > me)
        def _():
            kbuf[b] = jnp.zeros(k_ref.shape, BF16)
            vbuf[b] = jnp.zeros(v_ref.shape, BF16)

    row = lax.broadcasted_iota(jnp.int32, (slots, toks), 0)
    expert = jnp.zeros((slots, toks), jnp.int32)
    pos = row
    start, first_row = 0, 0
    for size in PARTS:
        for e in range(EXPERTS):
            here = row >= start + e * size
            expert = jnp.where(here, e, expert)
            pos = jnp.where(here, row - (start + e * size) + first_row, pos)
        start, first_row = start + EXPERTS * size, first_row + size
    token = lax.broadcasted_iota(jnp.int32, (slots, toks), 1)
    block_len = toks // 2
    in_second = (token >= block_len).astype(jnp.int32)
    ids = ids_ref[...]
    rw = rw_ref[...]
    first = jnp.where(ids[0:1, :] == expert, 1.0, 0.0)
    second = jnp.where(ids[1:2, :] == expert, 1.0, 0.0)
    chosen = first + second
    t_row = lax.broadcasted_iota(jnp.int32, (toks, toks), 0)
    t_col = lax.broadcasted_iota(jnp.int32, (toks, toks), 1)
    same = (t_row >= block_len) == (t_col >= block_len)
    upper = jnp.where(same & (t_row < t_col), 1.0, 0.0).astype(BF16)
    rank = jnp.dot(chosen.astype(BF16), upper, preferred_element_type=F32)
    wanted = (pos - in_second * HALF_CAP).astype(F32)
    placing = jnp.where(rank == wanted, chosen, 0.0)
    place[...] = placing.astype(BF16)
    weight = placing * (first * rw[0:1, :] + second * rw[1:2, :])
    high = weight.astype(BF16)
    comb[:, 0:toks] = high
    comb[:, toks:] = (weight - high.astype(F32)).astype(BF16)

    for dz in range(1, nz):
        @pl.when(level - dz >= 0)
        def _():
            block = me - 2 * dz
            for c in relay_copies(block, nz + dz - 1):
                c.wait_recv()
                c.start()
    for j in range(nz):
        block = 2 * j + 1 - parity

        @pl.when(block < me)
        def _():
            for c in relay_copies(block, 0):
                c.wait_recv()

    keys = n * toks
    q_pos = me * toks + lax.broadcasted_iota(jnp.int32, (toks, keys), 0)
    k_pos = lax.broadcasted_iota(jnp.int32, (toks, keys), 1)
    bias = jnp.where(k_pos <= q_pos, 0.0, -1e30)
    bias = jnp.concatenate([bias] * per_group, axis=0)
    scaling = HEAD_DIM ** (-0.5)
    squares = jnp.zeros((toks, 1), F32)
    for g in range(kv_local):
        head = slice(g * HEAD_DIM, (g + 1) * HEAD_DIM)
        base = g * per_group * HEAD_DIM
        qs = jnp.concatenate(
            [
                q_ref[:, base + j * HEAD_DIM : base + (j + 1) * HEAD_DIM]
                for j in range(per_group)
            ],
            axis=0,
        )
        ks = kbuf[:, :, head].reshape(keys, HEAD_DIM)
        vs = vbuf[:, :, head].reshape(keys, HEAD_DIM)
        s = lax.dot_general(qs, ks, (((1,), (1,)), ((), ())), preferred_element_type=F32)
        s = s * scaling + bias
        m = jnp.max(s, axis=1, keepdims=True)
        p = jnp.exp(s - m)
        total = jnp.sum(p, axis=1, keepdims=True)
        att = jnp.dot(p.astype(BF16), vs, preferred_element_type=F32) / total
        for j in range(per_group):
            cols = slice(base + j * HEAD_DIM, base + (j + 1) * HEAD_DIM)
            h = (res_ref[:, cols].astype(F32) + att[j * toks : (j + 1) * toks]).astype(BF16)
            hid[:, cols] = h
            squares = squares + jnp.sum(jnp.square(h.astype(F32)), axis=1, keepdims=True)

    sq_send[...] = jnp.broadcast_to(squares, sq_send.shape)
    sq_copy = pltpu.make_async_remote_copy(
        src_ref=sq_send, dst_ref=sq_recv, send_sem=sq_sem.at[0], recv_sem=sq_sem.at[1],
        device_id={"exp": sib}, device_id_type=MESH,
    )
    sq_copy.start()
    my_feat = pl.multiple_of(x * half_feat, half_feat)
    sib_feat = pl.multiple_of(sib * half_feat, half_feat)
    gain = gain_ref[:, pl.ds(my_feat, half_feat)]
    scaled = hid[...].astype(F32)
    sq_copy.wait()
    inv = lax.rsqrt((squares + sq_recv[:, 0:1]) / (2 * half_feat) + 1e-05)
    normed = (scaled * inv * gain).astype(BF16)

    sent = jnp.dot(place[...], normed, preferred_element_type=F32)
    my_expert = lax.div(me, spread)

    def disp_copy(p, dst, block, src_expert, slot):
        return pltpu.make_async_remote_copy(
            src_ref=send_buf[p].at[src_expert], dst_ref=recv_own[p].at[block],
            send_sem=disp_send.at[p, slot], recv_sem=disp_recv.at[p, block],
            device_id={"ctx": dst}, device_id_type=MESH,
        )

    def sib_copy(p, src, block):
        return pltpu.make_async_remote_copy(
            src_ref=src, dst_ref=recv_sib[p].at[block],
            send_sem=sib_send.at[p, block], recv_sem=sib_recv.at[p, block],
            device_id={"exp": sib}, device_id_type=MESH,
        )

    def p_copy(p, j):
        return pltpu.make_async_remote_copy(
            src_ref=psend[p].at[j], dst_ref=precv[p].at[j],
            send_sem=p_send.at[p, j], recv_sem=p_recv.at[p, j],
            device_id={"exp": sib}, device_id_type=MESH,
        )

    def r_copy(p, j, dst, block, slot):
        return pltpu.make_async_remote_copy(
            src_ref=rsend[p].at[j, dst], dst_ref=rrecv[p].at[j, block],
            send_sem=r_send.at[p, j, slot], recv_sem=r_recv.at[p, j, block],
            device_id={"ctx": dst}, device_id_type=MESH,
        )

    start = 0
    for p, size in enumerate(PARTS):
        part = sent[start : start + EXPERTS * size]
        start += EXPERTS * size
        send_buf[p][...] = part.reshape(EXPERTS, size, half_feat).astype(BF16)
        for m in order:
            dst = flip(m)
            disp_copy(p, dst, me, lax.div(dst, spread), m).start()
        sib_copy(p, send_buf[p].at[my_expert], me).start()
        recv_own[p][me] = send_buf[p][my_expert]

    for p, size in enumerate(PARTS):
        rows = n * size
        for m in order:
            src = flip(m)
            disp_copy(p, src, src, my_expert, m).wait_recv()
            sib_copy(p, recv_own[p].at[src], src).start()

        flat[0:rows, :] = recv_own[p][...].astype(F32).reshape(rows, half_feat).astype(BF16)
        if p == 0:
            wg_copy.wait()
        for c in range(ff // 256):
            cols = slice(c * 256, (c + 1) * 256)
            acc[0:rows, cols] = jnp.dot(
                flat[0:rows, :], wg[pl.ds(my_feat, half_feat), cols],
                preferred_element_type=F32,
            )
        for m in (0,) + tuple(order):
            sib_copy(p, send_buf[p].at[0], flip(m)).wait_recv()
        flat[0:rows, :] = recv_sib[p][...].astype(F32).reshape(rows, half_feat).astype(BF16)
        for c in range(ff // 256):
            cols = slice(c * 256, (c + 1) * 256)
            v = acc[0:rows, cols] + jnp.dot(
                flat[0:rows, :], wg[pl.ds(sib_feat, half_feat), cols],
                preferred_element_type=F32,
            )
            act[0:rows, cols] = (v / (1.0 + jnp.exp(-v))).astype(BF16)

        if p == 0:
            wd_copy.wait()
        for j in range(chunks):
            cols = pl.ds(pl.multiple_of(sib_feat + j * CHUNK, 128), CHUNK)
            y = jnp.dot(act[0:rows, :], wd[:, cols], preferred_element_type=F32)
            psend[p][j] = y.reshape(n, size, CHUNK).astype(BF16)
            p_copy(p, j).start()
        for j in range(chunks):
            cols = pl.ds(pl.multiple_of(my_feat + j * CHUNK, 128), CHUNK)
            y = jnp.dot(act[0:rows, :], wd[:, cols], preferred_element_type=F32)
            p_copy(p, j).wait_recv()
            rsend[p][j] = (y.reshape(n, size, CHUNK) + precv[p][j].astype(F32)).astype(BF16)
            for m in order:
                r_copy(p, j, flip(m), me, m).start()
            rrecv[p][j, me] = rsend[p][j, me]

    start = 0
    for p, size in enumerate(PARTS):
        lines = EXPERTS * size
        comb_part = comb[start : start + lines, :]
        start += lines
        for j in range(chunks):
            for m in order:
                src = flip(m)
                r_copy(p, j, src, src, m).wait_recv()
            back = rrecv[p][j].astype(F32).reshape(EXPERTS, spread, size, CHUNK)
            if spread == 1:
                terms = [back.reshape(lines, CHUNK).astype(BF16)]
            else:
                back = jnp.sum(back, axis=1).reshape(lines, CHUNK)
                top = back.astype(BF16)
                terms = [top, (back - top.astype(F32)).astype(BF16)]
            cols = slice(j * CHUNK, (j + 1) * CHUNK)
            mixed = branch[:, cols] if p else None
            for term in terms:
                both = lax.dot_general(
                    comb_part, term, (((0,), (0,)), ((), ())), preferred_element_type=F32
                )
                both = both[:toks] + both[toks:]
                mixed = both if mixed is None else mixed + both
            branch[:, cols] = mixed

    @pl.when(parity == 0)
    def _():
        for c in own_copies(partner, 0):
            c.wait_send()

    for dz in range(1, nz):
        @pl.when(level + dz < nz)
        def _():
            for c in own_copies(me + 2 * dz, dz):
                c.wait_send()

        @pl.when(level - dz >= 0)
        def _():
            for c in relay_copies(me - 2 * dz, nz + dz - 1):
                c.wait_send()

    for p in range(len(PARTS)):
        for m in order:
            dst = flip(m)
            disp_copy(p, dst, me, lax.div(dst, spread), m).wait_send()
        for m in (0,) + tuple(order):
            sib_copy(p, send_buf[p].at[0], flip(m)).wait_send()
        for j in range(chunks):
            p_copy(p, j).wait_send()
            for m in order:
                r_copy(p, j, flip(m), me, m).wait_send()


def solution(mesh):
    n = mesh.shape["ctx"]

    def body(q, k, v, res, gain, ids, rw, w_gate, w_down):
        toks, half_feat = q.shape
        ff = w_gate.shape[1]
        slots = EXPERTS * CAP
        chunks = half_feat // CHUNK
        parts = len(PARTS)
        most = n * max(PARTS)
        dma = pltpu.SemaphoreType.DMA
        vmem = pl.BlockSpec(memory_space=pltpu.VMEM)
        anyspace = pl.BlockSpec(memory_space=pl.ANY)
        by_part = lambda f: [pltpu.VMEM(f(size), BF16) for size in PARTS]
        hidden, branch = pl.pallas_call(
            functools.partial(kernel, n),
            out_shape=(
                jax.ShapeDtypeStruct((toks, half_feat), BF16),
                jax.ShapeDtypeStruct((toks, half_feat), F32),
            ),
            in_specs=[vmem] * 7 + [anyspace] * 2,
            out_specs=(vmem, vmem),
            scratch_shapes=[
                pltpu.VMEM((n, toks, k.shape[1]), BF16),
                pltpu.VMEM((n, toks, k.shape[1]), BF16),
                pltpu.VMEM(w_gate.shape, BF16),
                pltpu.VMEM(w_down.shape, BF16),
                pltpu.VMEM((slots, toks), BF16),
                pltpu.VMEM((slots, 2 * toks), BF16),
                pltpu.VMEM((toks, 128), F32),
                pltpu.VMEM((toks, 128), F32),
            ]
            + by_part(lambda size: (EXPERTS, size, half_feat))
            + by_part(lambda size: (n, size, half_feat))
            + by_part(lambda size: (n, size, half_feat))
            + [
                pltpu.VMEM((most, ff), F32),
                pltpu.VMEM((most, ff), BF16),
                pltpu.VMEM((most, half_feat), BF16),
            ]
            + by_part(lambda size: (chunks, n, size, CHUNK))
            + by_part(lambda size: (chunks, n, size, CHUNK))
            + by_part(lambda size: (chunks, n, size, CHUNK))
            + by_part(lambda size: (chunks, n, size, CHUNK))
            + [
                dma((2,)),
                dma((2, n)),
                dma((2, n)),
                dma((2,)),
                dma((parts, n)),
                dma((parts, n)),
                dma((parts, n)),
                dma((parts, n)),
                dma((parts, chunks)),
                dma((parts, chunks)),
                dma((parts, chunks, n)),
                dma((parts, chunks, n)),
            ],
            compiler_params=pltpu.CompilerParams(
                collective_id=0, has_side_effects=True, vmem_limit_bytes=56 * 1024 * 1024
            ),
        )(q, k, v, res, gain.reshape(1, -1), ids.T, rw.T, w_gate, w_down)
        return (hidden.astype(F32) + branch).astype(BF16)

    rows_spec = P(("groups", "ctx"), "exp")
    in_specs = (
        rows_spec, rows_spec, rows_spec, rows_spec, P(),
        P(("groups", "ctx"), None), P(("groups", "ctx"), None),
        P(None, ("ctx", "exp")), P(("ctx", "exp"), None),
    )
    return jax.shard_map(
        body, mesh=mesh, in_specs=in_specs, out_specs=rows_spec, check_vma=False
    )
```

time: 56.3 us -> 50.9 us (0.904)
  local copies, waits for them, and re-layouts: 4.36 us -> 0 us
  Pallas kernels: 51.7 us -> 49 us
  other arithmetic: 0 us -> 1.76 us
    unnamed x3 -> x0, local copies, waits for them, and re-layouts: 4.36 us -> none
    pallas_call x1, Pallas kernels: 51.7 us -> 49 us  [body(): pl.pallas_call(functools.partial(kernel, n), out_shape=(jax.ShapeDtypeStr...]
    convert_element_type x0 -> x1, other arithmetic: none -> 1.76 us  [body(): return (hidden.astype(F32) + branch).astype(BF16)]
where the time goes in v2:
time: 50.9 us; the launch traced here: 50.7 us
  Pallas kernels  49 us (96%)
  other arithmetic  1.76 us (3%)
    pallas_call x1, Pallas kernels, body(): pl.pallas_call(functools.partial(kernel, n), out_shape=(jax.ShapeDtypeStr...  49 us
    convert_element_type x1, other arithmetic, body(): return (hidden.astype(F32) + branch).astype(BF16)  1.76 us

profile of v2, /device:TPU:0, one launch (start us, length us, event | category | flops | bytes accessed | tf_op | source)
XLA Modules:
  0.0 50.7 jit_solution(13311898615266717309)
XLA Ops:
  0.0 49.0 %shard_map.91 = (bf16[64,1536]{1,0:T(8,128)(2,1)}, f32[64,1536]{1,0:T(8,128)}) custom-call(bf16[64,1536]{1,0:T(8,128)(2,1)} %q_ref.1, bf16[64,256]{1,0:T(8,128)(2,1)} %k_ref.1, bf16[64,256]{1,0:T(8,128)(2,1)} %v_ref.1, bf16[64,1536]{1,0:T(8,128)(2,1)} %res_ref.1, f32[1,3072]{1,0:T(1,128)} %bitcast.3, s32[2,64]{1,0:T(2,128)} %bitcast.4, f32[2,64]{1,0:T(2,128)} %bitcast.5, ...), custom_call_target="tpu_custom_call" | custom-call | tf_op jit(solution)/shard_map/pallas_call | solution.py:354
  49.0 1.8 %add_convert_fusion = bf16[64,1536]{1,0:T(8,128)(2,1)} fusion(f32[64,1536]{1,0:T(8,128)} %get-tuple-element.8, bf16[64,1536]{1,0:T(8,128)(2,1)} %get-tuple-element.7), kind=kLoop, calls=%fused_computation | loop fusion | flops 294912 | bytes 786432 | tf_op jit(solution)/shard_map/convert_element_type | solution.py:402

commit v3 on v2

--- a/solution.py
+++ b/solution.py
@@ -11,7 +11,7 @@
 EXPERTS = 8
 HALF_CAP = 12
 CAP = 2 * HALF_CAP
-PARTS = (16, 8)
+PARTS = (8, 16)
 CHUNK = 768
 MESH = pl.DeviceIdType.MESH
 F32 = jnp.float32
@@ -20,8 +20,9 @@
 
 def kernel(
     n,
-    q_ref, k_ref, v_ref, res_ref, gain_ref, ids_ref, rw_ref, wg_hbm, wd_hbm,
-    hid, branch,
+    q_hbm, k_ref, v_ref, res_hbm, gain_hbm, ids_hbm, rw_hbm, wg_hbm, wd_hbm,
+    out_ref,
+    hid, branch, q_ref, res_ref, gain_ref, ids_ref, rw_ref, in_sem,
     kbuf, vbuf, wg, wd, place, comb, sq_send, sq_recv,
     send_a, send_b, own_a, own_b, other_a, other_b, acc, act, flat,
     psend_a, psend_b, precv_a, precv_b, rsend_a, rsend_b, rrecv_a, rrecv_b,
@@ -56,6 +57,17 @@
 
     wg_copy = pltpu.make_async_copy(wg_hbm, wg, w_sem.at[0])
     wd_copy = pltpu.make_async_copy(wd_hbm, wd, w_sem.at[1])
+    loads = [
+        pltpu.make_async_copy(src, dst, in_sem.at[i])
+        for i, (src, dst) in enumerate(
+            (
+                (ids_hbm, ids_ref), (rw_hbm, rw_ref), (k_ref, kbuf.at[me]), (v_ref, vbuf.at[me]),
+                (q_hbm, q_ref), (res_hbm, res_ref), (gain_hbm, gain_ref),
+            )
+        )
+    ]
+    for load in loads:
+        load.start()
     wg_copy.start()
     wd_copy.start()
 
@@ -99,8 +111,6 @@
             for c in own_copies(me + 2 * dz, dz):
                 c.start()
 
-    kbuf[me] = k_ref[...]
-    vbuf[me] = v_ref[...]
     for b in range(n):
         @pl.when(b > me)
         def _():
@@ -120,6 +130,8 @@
     token = lax.broadcasted_iota(jnp.int32, (slots, toks), 1)
     block_len = toks // 2
     in_second = (token >= block_len).astype(jnp.int32)
+    loads[0].wait()
+    loads[1].wait()
     ids = ids_ref[...]
     rw = rw_ref[...]
     first = jnp.where(ids[0:1, :] == expert, 1.0, 0.0)
@@ -153,6 +165,8 @@
             for c in relay_copies(block, 0):
                 c.wait_recv()
 
+    for load in loads[2:]:
+        load.wait()
     keys = n * toks
     q_pos = me * toks + lax.broadcasted_iota(jnp.int32, (toks, keys), 0)
     k_pos = lax.broadcasted_iota(jnp.int32, (toks, keys), 1)
@@ -307,7 +321,10 @@
                 )
                 both = both[:toks] + both[toks:]
                 mixed = both if mixed is None else mixed + both
-            branch[:, cols] = mixed
+            if p < len(PARTS) - 1:
+                branch[:, cols] = mixed
+            else:
+                out_ref[:, cols] = (hid[:, cols].astype(F32) + mixed).astype(BF16)
 
     @pl.when(parity == 0)
     def _():
@@ -349,17 +366,21 @@
         most = n * max(PARTS)
         dma = pltpu.SemaphoreType.DMA
         vmem = pl.BlockSpec(memory_space=pltpu.VMEM)
-        anyspace = pl.BlockSpec(memory_space=pl.ANY)
         by_part = lambda f: [pltpu.VMEM(f(size), BF16) for size in PARTS]
-        hidden, branch = pl.pallas_call(
+        return pl.pallas_call(
             functools.partial(kernel, n),
-            out_shape=(
-                jax.ShapeDtypeStruct((toks, half_feat), BF16),
-                jax.ShapeDtypeStruct((toks, half_feat), F32),
-            ),
-            in_specs=[vmem] * 7 + [anyspace] * 2,
-            out_specs=(vmem, vmem),
+            out_shape=jax.ShapeDtypeStruct((toks, half_feat), BF16),
+            in_specs=[pl.BlockSpec(memory_space=pltpu.HBM)] * 9,
+            out_specs=vmem,
             scratch_shapes=[
+                pltpu.VMEM(q.shape, BF16),
+                pltpu.VMEM(q.shape, F32),
+                pltpu.VMEM(q.shape, BF16),
+                pltpu.VMEM(res.shape, BF16),
+                pltpu.VMEM((1, gain.shape[0]), F32),
+                pltpu.VMEM(ids.T.shape, jnp.int32),
+                pltpu.VMEM(rw.T.shape, F32),
+                dma((7,)),
                 pltpu.VMEM((n, toks, k.shape[1]), BF16),
                 pltpu.VMEM((n, toks, k.shape[1]), BF16),
                 pltpu.VMEM(w_gate.shape, BF16),
@@ -399,7 +420,6 @@
                 collective_id=0, has_side_effects=True, vmem_limit_bytes=56 * 1024 * 1024
             ),
         )(q, k, v, res, gain.reshape(1, -1), ids.T, rw.T, w_gate, w_down)
-        return (hidden.astype(F32) + branch).astype(BF16)
 
     rows_spec = P(("groups", "ctx"), "exp")
     in_specs = (

time: 50.9 us -> 49.3 us (0.969)
  other arithmetic: 1.76 us -> 0 us
  local copies, waits for them, and re-layouts: 0 us -> 1.62 us
  Pallas kernels: 49 us -> 47.5 us
    convert_element_type x1 -> x0, other arithmetic: 1.76 us -> none  [body(): return (hidden.astype(F32) + branch).astype(BF16)]
    unnamed x0 -> x1, local copies, waits for them, and re-layouts: none -> 1.62 us
    pallas_call x1, Pallas kernels: 49 us -> 47.5 us  [body(): pl.pallas_call(functools.partial(kernel, n), out_shape=jax.ShapeDtypeStru...]
where the time goes in v3:
time: 49.3 us; the launch traced here: 49.1 us
  Pallas kernels  47.5 us (96%)
  local copies, waits for them, and re-layouts  1.62 us (3%)
    pallas_call x1, Pallas kernels, body(): pl.pallas_call(functools.partial(kernel, n), out_shape=jax.ShapeDtypeStru...  47.5 us
    unnamed x1, local copies, waits for them, and re-layouts  1.62 us

profile of v3, /device:TPU:0, one launch (start us, length us, event | category | flops | bytes accessed | tf_op | source)
XLA Modules:
  0.0 49.1 jit_solution(17865210144086675288)
XLA Ops:
  0.0 47.5 %shard_map.91 = bf16[64,1536]{1,0:T(8,128)(2,1)} custom-call(bf16[64,1536]{1,0:T(8,128)(2,1)} %q_hbm.1, bf16[64,256]{1,0:T(8,128)(2,1)} %k_ref.1, bf16[64,256]{1,0:T(8,128)(2,1)} %v_ref.1, bf16[64,1536]{1,0:T(8,128)(2,1)} %res_hbm.1, f32[1,3072]{1,0:T(1,128)} %bitcast.3, s32[2,64]{1,0:T(2,128)} %bitcast.4, f32[2,64]{1,0:T(2,128)} %bitcast.5, ...), custom_call_target="tpu_custom_call" | custom-call | tf_op jit(solution)/shard_map/pallas_call | solution.py:370
  47.5 1.6 %copy.11 = bf16[64,1536]{1,0:T(8,128)(2,1)} copy(bf16[64,1536]{1,0:T(8,128)(2,1)} %shard_map.91) | data formatting | bytes 393216
